TPU v7x, 32 devices: a whole 2x2x4 slice. The times are simulated.
32 devices in a mesh: dp: 8 (over y, x, core), chan: 4 (over z).
Axes of the slice: x: 2, y: 2, z: 4, core: 2. Of those that a mesh axis runs over, the one named last changes fastest.
Arguments:
- patches: bfloat16 [64, 256, 1280], P('dp', None, 'chan'), may hold values from -13 to 13
- cotangent: bfloat16 [64, 256, 1280], P('dp', None, 'chan'), may hold values from -33 to 33
- w_token_in: bfloat16 [640, 256], replicated, may hold values from -0.375 to 0.375
- b_token_in: float32 [640], replicated, may hold values from -3 to 3
- w_token_out: bfloat16 [256, 640], replicated, may hold values from -0.25 to 0.25
- layer_norm_gain: float32 [1280], replicated, may hold values from 0.25 to 1.75
- layer_norm_bias: float32 [1280], replicated, may hold values from -3 to 3
Outputs:
- grad_patches: bfloat16 [64, 256, 1280], P('dp', None, 'chan')
- grad_w_in: float32 [640, 256], replicated
- grad_w_out: float32 [256, 640], replicated
- grad_b_in: float32 [640], replicated
- grad_gain: float32 [1280], P('chan')
- grad_shift: float32 [1280], P('chan')
All inputs are finite; a program needn't handle non-finite values.
Results may differ from a plain program's by a relative error of at most 0.0065.
Values may be sent and summed in bfloat16 or wider, within the bound.
No kernel may reach another device: no remote copies, remote signals or barrier semaphores. Data moves between devices by JAX's collectives and lax.ppermute only.
A program may use at most 64 MiB of HBM per device.

v0:
```python
import math
import jax
import jax.numpy as jnp
from jax import lax
from jax.sharding import PartitionSpec as P

CHANNEL_COUNT = 1280
eps_norm = 1e-05


def shards(
    patches, cotangent, w_token_in, b_token_in, w_token_out, layer_norm_gain, layer_norm_bias
):
    where = lax.axis_index("chan")
    local_width = patches.shape[2]
    images = float(patches.shape[0] * lax.axis_size("dp"))
    input_float = patches.astype(jnp.float32)
    totals = lax.psum((jnp.sum(input_float, -1), jnp.sum(input_float * input_float, -1)), "chan")
    row_average = totals[0] / CHANNEL_COUNT
    inverse_deviation = lax.rsqrt(totals[1] / CHANNEL_COUNT - row_average * row_average + eps_norm)
    local_gain = lax.dynamic_slice_in_dim(layer_norm_gain, where * local_width, local_width, 0)
    local_bias = lax.dynamic_slice_in_dim(layer_norm_bias, where * local_width, local_width, 0)
    centered_input = (input_float - row_average[..., None]) * inverse_deviation[..., None]
    normalized_output = (centered_input * local_gain + local_bias).astype(jnp.bfloat16)
    pre = (
        jnp.einsum("kp,bpc->bkc", w_token_in, normalized_output, preferred_element_type=jnp.float32)
        + b_token_in[None, :, None]
    )
    cdf = 0.5 * (1.0 + jax.scipy.special.erf(pre / math.sqrt(2.0)))
    act = (pre * cdf).astype(jnp.bfloat16)
    slope = cdf + pre * jnp.exp(-0.5 * pre * pre) / math.sqrt(2.0 * math.pi)
    grad_act = jnp.einsum("pk,bpc->bkc", w_token_out, cotangent, preferred_element_type=jnp.float32)
    grad_pre = (grad_act * slope).astype(jnp.bfloat16)
    gradient_normalized = jnp.einsum(
        "kp,bkc->bpc", w_token_in, grad_pre, preferred_element_type=jnp.float32
    ).astype(jnp.bfloat16)
    dw_out = jnp.einsum("bpc,bkc->pk", cotangent, act, preferred_element_type=jnp.float32)
    dw_in = jnp.einsum(
        "bkc,bpc->kp", grad_pre, normalized_output, preferred_element_type=jnp.float32
    )
    db_in = jnp.sum(grad_pre.astype(jnp.float32), axis=(0, 2))
    summed = lax.psum((dw_in, dw_out, db_in), ("dp", "chan"))
    gradient_block = gradient_normalized.astype(jnp.float32)
    norm_terms = lax.psum(
        (
            jnp.sum(gradient_block * centered_input, axis=(0, 1)),
            jnp.sum(gradient_block, axis=(0, 1)),
        ),
        "dp",
    )
    gradient_centered = gradient_block * local_gain
    sums = lax.psum(
        (jnp.sum(gradient_centered, -1), jnp.sum(gradient_centered * centered_input, -1)), "chan"
    )
    first_term = sums[0] / CHANNEL_COUNT
    second_term = sums[1] / CHANNEL_COUNT
    result = cotangent.astype(jnp.float32) + inverse_deviation[..., None] * (
        gradient_centered - first_term[..., None] - centered_input * second_term[..., None]
    )
    grad_patches = result.astype(jnp.bfloat16)
    return (
        grad_patches,
        summed[0] / images,
        summed[1] / images,
        summed[2] / images,
        norm_terms[0] / images,
        norm_terms[1] / images,
    )


def solution(mesh):
    placed = (P("dp", None, "chan"), P("dp", None, "chan"), P(), P(), P(), P(), P())
    return jax.shard_map(
        shards,
        mesh=mesh,
        in_specs=placed,
        out_specs=(P("dp", None, "chan"), P(), P(), P(), P("chan"), P("chan")),
        check_vma=False,
    )
```

profile of v0, /device:TPU:0, one launch (start us, length us, event | category | flops | bytes accessed | tf_op | source)
XLA Modules:
  0.0 185.8 jit_solution(13512092511223534403)
XLA Ops:
  7.2 0.0 copy-start
  7.2 0.0 all-reduce.6.cloned.1.call-start
  7.2 0.8 dynamic_slice.6
  8.0 0.8 dynamic_slice.7
  8.8 1.7 fusion.24
  10.5 20.5 %all-reduce.3 = (f32[8,256]{1,0:T(8,128)S(1)}, f32[8,256]{1,0:T(8,128)S(1)}) all-reduce(f32[8,256]{1,0:T(8,128)S(1)} %get-tuple-element.16, f32[8,256]{1,0:T(8,128)S(1)} %get-tuple-element.15), channel_id=1, replica_groups=mesh['dp'=8,'chan'=4] {'chan'}, use_global_device_ids=true, to_apply=%region_3.0 | all-reduce | flops 4096 | bytes 32768 | tf_op jit(solution)/shard_map/psum | solution.py:18
  31.0 0.0 copy-done
  31.0 0.0 copy-start.2
  31.1 0.0 copy-start.4
  31.1 2.7 %fusion.34 = f32[8,320,640]{2,1,0:T(8,128)S(1)} fusion(bf16[640,256]{1,0:T(8,128)(2,1)S(1)} %copy-done, bf16[8,256,320]{1,2,0:T(8,128)(2,1)} %param.7, f32[320]{0:T(512)S(1)} %dynamic_slice.7, f32[320]{0:T(512)S(1)} %dynamic_slice.6, f32[8,256]{1,0:T(8,128)S(1)} %get-tuple-element.26, f32[8,256]{1,0:T(8,128)S(1)} %get-tuple-element.25), kind=kOutput, calls=%fused_computation.42 | convolution fusion | flops 842792960 | bytes 8210944 | tf_op jit(solution)/shard_map/kp,bpc->bkc/dot_general | solution.py:26
  33.8 0.0 copy-done.2
  33.8 0.0 copy-done.4
  33.8 0.0 copy-start.3
  33.8 2.4 %fusion.30 = f32[256,640]{0,1:T(8,128)} fusion(bf16[8,256,320]{1,2,0:T(8,128)(2,1)S(1)} %copy-done.2, f32[8,320,640]{2,1,0:T(8,128)S(1)} %fusion.34, f32[640]{0:T(1024)S(1)} %copy-done.4), kind=kOutput, calls=%fused_computation.39 | convolution fusion | flops 848691200 | bytes 8522240 | tf_op jit(solution)/shard_map/bpc,bkc->pk/dot_general | solution.py:37
  36.3 0.0 copy-done.3
  36.3 0.0 copy-start.1
  36.3 3.8 %convert_reduce_fusion = (f32[640]{0:T(1024)S(1)}, bf16[8,640,320]{1,2,0:T(8,128)(2,1)S(1)}) fusion(f32[8,320,640]{2,1,0:T(8,128)S(1)} %fusion.34, f32[640]{0:T(1024)S(1)} %copy-done.4, bf16[8,256,320]{1,2,0:T(8,128)(2,1)S(1)} %copy-done.2, bf16[256,640]{1,0:T(8,128)(2,1)S(1)} %copy-done.3), kind=kOutput, calls=%fused_computation.13 | convolution fusion | flops 860159360 | bytes 11473920 | tf_op jit(solution)/shard_map/pk,bpc->bkc/dot_general | solution.py:32
  40.1 0.0 copy-start.5
  40.1 1.7 copy-done.5
  41.8 0.0 copy-done.1
  41.8 2.1 %convolution_bitcast_fusion = f32[640,256]{1,0:T(8,128)} fusion(bf16[8,640,320]{1,2,0:T(8,128)(2,1)S(1)} %get-tuple-element.29, bf16[8,256,320]{1,2,0:T(8,128)(2,1)S(1)} %copy-done.1, f32[320]{0:T(512)S(1)} %dynamic_slice.7, f32[320]{0:T(512)S(1)} %dynamic_slice.6, f32[8,256]{1,0:T(8,128)S(1)} %get-tuple-element.26, f32[8,256]{1,0:T(8,128)S(1)} %get-tuple-element.25), kind=kOutput, calls=%fused_computation.40 | convolution fusion | flops 842792960 | bytes 5261824 | tf_op jit(solution)/shard_map/bkc,bpc->kp/dot_general | solution.py:38
  43.9 0.0 all-reduce.6.cloned.1.call-update
  43.9 3.5 %fusion.23 = (f32[320]{0:T(512)S(1)}, f32[8,256]{1,0:T(8,128)S(1)}, f32[8,256]{1,0:T(8,128)S(1)}, bf16[8,320,256]{2,1,0:T(8,128)(2,1)S(1)}) fusion(bf16[8,256,320]{1,2,0:T(8,128)(2,1)S(1)} %copy-done.1, f32[8,256]{1,0:T(8,128)S(1)} %get-tuple-element.26, f32[8,256]{1,0:T(8,128)S(1)} %get-tuple-element.25, f32[320]{0:T(512)S(1)} %dynamic_slice.6, ...), kind=kOutput, calls=%fused_computation.31 | convolution fusion | flops 846065344 | bytes 6261248 | tf_op jit(solution)/shard_map/kp,bkc->bpc/dot_general | solution.py:34
  47.5 38.1 %psum.69 = f32[640]{0:T(1024)S(1)} all-reduce(f32[640]{0:T(1024)S(1)} %get-tuple-element.28), channel_id=1, replica_groups=mesh['dp'=8,'chan'=4] {'dp','chan'}, use_global_device_ids=true, to_apply=%region_11.0 | all-reduce | flops 640 | bytes 5120 | tf_op jit(solution)/shard_map/psum | solution.py:42
  85.5 0.6 broadcast_multiply_fusion.5
  86.1 0.3 convert_reduce_fusion.2
  86.4 12.7 %all-reduce.1 = (f32[320]{0:T(512)S(1)}, f32[320]{0:T(512)S(1)}) all-reduce(f32[320]{0:T(512)S(1)} %get-tuple-element.12, f32[320]{0:T(512)S(1)} %convert_reduce_fusion.2), channel_id=1, replica_groups=mesh['dp'=8,'chan'=4] {'dp'}, use_global_device_ids=true, to_apply=%region_13.0 | all-reduce | flops 640 | bytes 5120 | tf_op jit(solution)/shard_map/psum | solution.py:44
  99.1 0.6 broadcast_multiply_fusion.6
  99.7 18.1 %all-reduce.2 = (f32[8,256]{1,0:T(8,128)S(1)}, f32[8,256]{1,0:T(8,128)S(1)}) all-reduce(f32[8,256]{1,0:T(8,128)S(1)} %get-tuple-element.13, f32[8,256]{1,0:T(8,128)S(1)} %get-tuple-element.14), channel_id=1, replica_groups=mesh['dp'=8,'chan'=4] {'chan'}, use_global_device_ids=true, to_apply=%region_7.0 | all-reduce | flops 4096 | bytes 32768 | tf_op jit(solution)/shard_map/psum | solution.py:52
  117.8 3.4 %fusion.21 = bf16[8,256,320]{1,2,0:T(8,128)(2,1)} fusion(bf16[8,320,256]{2,1,0:T(8,128)(2,1)S(1)} %get-tuple-element.27, bf16[8,256,320]{1,2,0:T(8,128)(2,1)S(1)} %copy-done.1, bf16[8,256,320]{1,2,0:T(8,128)(2,1)} %param.8, f32[8,256]{1,0:T(8,128)S(1)} %get-tuple-element.30, f32[8,256]{1,0:T(8,128)S(1)} %get-tuple-element.31, f32[320]{0:T(512)S(1)} %dynamic_slice.6, ...), kind=kLoop, calls=%fused_computation.29 | loop fusion | flops 7864320 | bytes 5276928 | tf_op jit(solution)/shard_map/convert_element_type | solution.py:60
  121.3 53.5 %all-reduce.6.cloned.1.call-done = (f32[640,256]{1,0:T(8,128)}, f32[256,640]{0,1:T(8,128)}) async-done(((f32[640,256]{1,0:T(8,128)}, f32[256,640]{0,1:T(8,128)}), (f32[640,256]{1,0:T(8,128)}, f32[256,640]{0,1:T(8,128)})) %all-reduce.6.cloned.1.call-update) | async-done | bytes 1310736 | tf_op jit(solution)/shard_map/psum | solution.py:42
  174.8 2.0 %broadcast_multiply_fusion.1 = f32[640,256]{1,0:T(8,128)} fusion(f32[640,256]{1,0:T(8,128)} %get-tuple-element.17), kind=kLoop, calls=%fused_computation.46 | loop fusion | flops 163840 | bytes 1310720 | tf_op jit(solution)/shard_map/div | solution.py:63
  176.8 1.1 broadcast_multiply_fusion
  177.9 1.1 copy.13
  (2 shorter events, 0.0 us)
Async XLA Ops:
  7.2 23.9 %copy-start = (bf16[640,256]{1,0:T(8,128)(2,1)S(1)}, bf16[640,256]{1,0:T(8,128)(2,1)}, u32[]{:S(2)}) copy-start(bf16[640,256]{1,0:T(8,128)(2,1)} %param.9) | copy-start | bytes 983044
  7.2 167.6 %all-reduce.6.cloned.1.call-start = ((), (), s32[]{:S(2)}) async-start(), calls=%async_computation | async-start | bytes 2621440 | tf_op jit(solution)/shard_map/psum | solution.py:42
  31.0 2.8 %copy-start.2 = (bf16[8,256,320]{1,2,0:T(8,128)(2,1)S(1)}, bf16[8,256,320]{1,2,0:T(8,128)(2,1)}, u32[]{:S(2)}) copy-start(bf16[8,256,320]{1,2,0:T(8,128)(2,1)} %param.8) | copy-start | bytes 3932164
  31.1 2.8 %copy-start.4 = (f32[640]{0:T(1024)S(1)}, f32[640]{0:T(1024)}, u32[]{:S(2)}) copy-start(f32[640]{0:T(1024)} %param.10) | copy-start | bytes 7684
  33.8 2.4 %copy-start.3 = (bf16[256,640]{1,0:T(8,128)(2,1)S(1)}, bf16[256,640]{1,0:T(8,128)(2,1)}, u32[]{:S(2)}) copy-start(bf16[256,640]{1,0:T(8,128)(2,1)} %param.11) | copy-start | bytes 983044
  36.3 5.5 %copy-start.1 = (bf16[8,256,320]{1,2,0:T(8,128)(2,1)S(1)}, bf16[8,256,320]{1,2,0:T(8,128)(2,1)}, u32[]{:S(2)}) copy-start(bf16[8,256,320]{1,2,0:T(8,128)(2,1)} %param.7) | copy-start | bytes 3932164
  40.1 1.7 copy-start.5
Sparse Core Ops, SparseCore 0:
  44.1 130.7 all-reduce.5
where the time goes:
time: 186 us
  blocking collectives  89.4 us (48%)
  waiting for transfers between devices  53.5 us (29%)
  matrix products  14.6 us (8%)
  between operations  14.1 us (8%)
  other arithmetic  9.7 us (5%)
  local copies, waits for them, and re-layouts  4.36 us (2%)
    psum x1, waiting for transfers between devices, shards(): summed = lax.psum((dw_in, dw_out, db_in), ('dp', 'chan'))  53.5 us
    psum x1, blocking collectives, shards(): summed = lax.psum((dw_in, dw_out, db_in), ('dp', 'chan'))  38.1 us
    psum x1, blocking collectives, shards(): lax.psum((jnp.sum(input_float, -1), jnp.sum(input_float * input_float, -1...  20.5 us
    psum x1, blocking collectives, shards(): lax.psum((jnp.sum(gradient_centered, -1), jnp.sum(gradient_centered * cen...  18.1 us
    psum x1, blocking collectives, shards(): lax.psum((jnp.sum(gradient_block * centered_input, axis=(0, 1)), jnp.sum(...  12.7 us
    dot_general x1, matrix products, shards(): jnp.einsum('pk,bpc->bkc', w_token_out, cotangent, preferred_element_type=...  3.83 us
  transfers between devices with their start and end apart: 1, of which 1 were waited for; matrix products, arithmetic and copies ran while one was open for 5% of the time, Pallas kernels for 0%

commit v1 on v0

--- a/solution.py
+++ b/solution.py
@@ -39,7 +39,7 @@
         "bkc,bpc->kp", grad_pre, normalized_output, preferred_element_type=jnp.float32
     )
     db_in = jnp.sum(grad_pre.astype(jnp.float32), axis=(0, 2))
-    summed = lax.psum((dw_in, dw_out, db_in), ("dp", "chan"))
+    summed = lax.psum(lax.psum((dw_in, dw_out, db_in), "chan"), "dp")
     gradient_block = gradient_normalized.astype(jnp.float32)
     norm_terms = lax.psum(
         (

time: 186 us -> 175 us (0.941)
  blocking collectives: 89.4 us -> 50.3 us
  waiting for transfers between devices: 53.5 us -> 81.8 us
    psum x2 -> x1, blocking collectives: 50.8 us -> 12.4 us  [shards(): summed = lax.psum(lax.psum((dw_in, dw_out, db_in), 'chan'), 'dp')]
    psum x1 -> x2, waiting for transfers between devices: 53.5 us -> 81.8 us  [shards(): summed = lax.psum(lax.psum((dw_in, dw_out, db_in), 'chan'), 'dp')]
  transfers between devices with their start and end apart: 1 -> 2, of which waited for: 1 -> 2; matrix products, arithmetic and copies ran while one was open for 5% -> 5% of each run, Pallas kernels for 0% -> 0%
where the time goes in v1:
time: 175 us
  waiting for transfers between devices  81.8 us (47%)
  blocking collectives  50.3 us (29%)
  matrix products  14.6 us (8%)
  between operations  14.1 us (8%)
  other arithmetic  9.69 us (6%)
  local copies, waits for them, and re-layouts  4.36 us (2%)
    psum x2, waiting for transfers between devices, shards(): summed = lax.psum(lax.psum((dw_in, dw_out, db_in), 'chan'), 'dp')  81.8 us
    psum x1, blocking collectives, shards(): lax.psum((jnp.sum(input_float, -1), jnp.sum(input_float * input_float, -1...  20.5 us
    psum x1, blocking collectives, shards(): lax.psum((jnp.sum(gradient_centered, -1), jnp.sum(gradient_centered * cen...  17.4 us
    psum x1, blocking collectives, shards(): summed = lax.psum(lax.psum((dw_in, dw_out, db_in), 'chan'), 'dp')  12.4 us
    dot_general x1, matrix products, shards(): jnp.einsum('pk,bpc->bkc', w_token_out, cotangent, preferred_element_type=...  3.81 us
    dot_general x1, matrix products, shards(): jnp.einsum('kp,bkc->bpc', w_token_in, grad_pre, preferred_element_type=jn...  3.55 us
  transfers between devices with their start and end apart: 2, of which 2 were waited for; matrix products, arithmetic and copies ran while one was open for 5% of the time, Pallas kernels for 0%

profile of v1, /device:TPU:0, one launch (start us, length us, event | category | flops | bytes accessed | tf_op | source)
XLA Modules:
  0.0 175.0 jit_solution(9042718723528089847)
XLA Ops:
  7.2 0.0 copy-start
  7.2 0.0 all-reduce.10.cloned.1.call-start
  7.2 0.8 dynamic_slice.6
  8.0 0.8 dynamic_slice.7
  8.8 1.7 fusion.24
  10.5 20.5 %all-reduce.3 = (f32[8,256]{1,0:T(8,128)S(1)}, f32[8,256]{1,0:T(8,128)S(1)}) all-reduce(f32[8,256]{1,0:T(8,128)S(1)} %get-tuple-element.16, f32[8,256]{1,0:T(8,128)S(1)} %get-tuple-element.15), channel_id=1, replica_groups=mesh['dp'=8,'chan'=4] {'chan'}, use_global_device_ids=true, to_apply=%region_3.0 | all-reduce | flops 4096 | bytes 32768 | tf_op jit(solution)/shard_map/psum | solution.py:18
  31.0 0.0 copy-done
  31.0 0.0 copy-start.2
  31.1 0.0 copy-start.4
  31.1 2.7 %fusion.34 = f32[8,320,640]{2,1,0:T(8,128)S(1)} fusion(bf16[640,256]{1,0:T(8,128)(2,1)S(1)} %copy-done, bf16[8,256,320]{1,2,0:T(8,128)(2,1)} %param.7, f32[320]{0:T(512)S(1)} %dynamic_slice.7, f32[320]{0:T(512)S(1)} %dynamic_slice.6, f32[8,256]{1,0:T(8,128)S(1)} %get-tuple-element.30, f32[8,256]{1,0:T(8,128)S(1)} %get-tuple-element.29), kind=kOutput, calls=%fused_computation.42 | convolution fusion | flops 842792960 | bytes 8210944 | tf_op jit(solution)/shard_map/kp,bpc->bkc/dot_general | solution.py:26
  33.8 0.0 copy-done.2
  33.8 0.0 copy-done.4
  33.8 0.0 copy-start.3
  33.8 2.4 %fusion.30 = f32[256,640]{0,1:T(8,128)} fusion(bf16[8,256,320]{1,2,0:T(8,128)(2,1)S(1)} %copy-done.2, f32[8,320,640]{2,1,0:T(8,128)S(1)} %fusion.34, f32[640]{0:T(1024)S(1)} %copy-done.4), kind=kOutput, calls=%fused_computation.39 | convolution fusion | flops 848691200 | bytes 8522240 | tf_op jit(solution)/shard_map/bpc,bkc->pk/dot_general | solution.py:37
  36.3 0.0 copy-done.3
  36.3 0.0 copy-start.1
  36.3 3.8 %convert_reduce_fusion = (f32[640]{0:T(1024)S(1)}, bf16[8,640,320]{1,2,0:T(8,128)(2,1)S(1)}) fusion(f32[8,320,640]{2,1,0:T(8,128)S(1)} %fusion.34, f32[640]{0:T(1024)S(1)} %copy-done.4, bf16[8,256,320]{1,2,0:T(8,128)(2,1)S(1)} %copy-done.2, bf16[256,640]{1,0:T(8,128)(2,1)S(1)} %copy-done.3), kind=kOutput, calls=%fused_computation.13 | convolution fusion | flops 860159360 | bytes 11473920 | tf_op jit(solution)/shard_map/pk,bpc->bkc/dot_general | solution.py:32
  40.1 0.0 copy-start.5
  40.1 1.7 copy-done.5
  41.8 0.0 copy-done.1
  41.8 2.1 %convolution_bitcast_fusion = f32[640,256]{1,0:T(8,128)} fusion(bf16[8,640,320]{1,2,0:T(8,128)(2,1)S(1)} %get-tuple-element.33, bf16[8,256,320]{1,2,0:T(8,128)(2,1)S(1)} %copy-done.1, f32[320]{0:T(512)S(1)} %dynamic_slice.7, f32[320]{0:T(512)S(1)} %dynamic_slice.6, f32[8,256]{1,0:T(8,128)S(1)} %get-tuple-element.30, f32[8,256]{1,0:T(8,128)S(1)} %get-tuple-element.29), kind=kOutput, calls=%fused_computation.40 | convolution fusion | flops 842792960 | bytes 5261824 | tf_op jit(solution)/shard_map/bkc,bpc->kp/dot_general | solution.py:38
  43.9 0.0 all-reduce.10.cloned.1.call-update
  43.9 0.0 all-reduce.8.cloned.1.call-start
  44.0 3.5 %fusion.23 = (f32[320]{0:T(512)S(1)}, f32[8,256]{1,0:T(8,128)S(1)}, f32[8,256]{1,0:T(8,128)S(1)}, bf16[8,320,256]{2,1,0:T(8,128)(2,1)S(1)}) fusion(bf16[8,256,320]{1,2,0:T(8,128)(2,1)S(1)} %copy-done.1, f32[8,256]{1,0:T(8,128)S(1)} %get-tuple-element.30, f32[8,256]{1,0:T(8,128)S(1)} %get-tuple-element.29, f32[320]{0:T(512)S(1)} %dynamic_slice.6, ...), kind=kOutput, calls=%fused_computation.31 | convolution fusion | flops 846065344 | bytes 6261248 | tf_op jit(solution)/shard_map/kp,bkc->bpc/dot_general | solution.py:34
  47.5 17.4 %all-reduce.2 = (f32[8,256]{1,0:T(8,128)S(1)}, f32[8,256]{1,0:T(8,128)S(1)}, f32[640]{0:T(1024)S(1)}) all-reduce(f32[8,256]{1,0:T(8,128)S(1)} %get-tuple-element.13, f32[8,256]{1,0:T(8,128)S(1)} %get-tuple-element.14, f32[640]{0:T(1024)S(1)} %get-tuple-element.32), channel_id=1, replica_groups=mesh['dp'=8,'chan'=4] {'chan'}, use_global_device_ids=true, to_apply=%region_7.0 | all-reduce | flops 4736 | bytes 37888 | tf_op jit(solution)/shard_map/psum | solution.py:52
  64.9 0.3 convert_reduce_fusion.2
  65.2 12.4 %all-reduce = (f32[640]{0:T(1024)S(1)}, f32[320]{0:T(512)S(1)}, f32[320]{0:T(512)S(1)}) all-reduce(f32[640]{0:T(1024)S(1)} %get-tuple-element.24, f32[320]{0:T(512)S(1)} %get-tuple-element.12, f32[320]{0:T(512)S(1)} %convert_reduce_fusion.2), channel_id=1, replica_groups=mesh['dp'=8,'chan'=4] {'dp'}, use_global_device_ids=true, to_apply=%region_14.0 | all-reduce | flops 1280 | bytes 10240 | tf_op jit(solution)/shard_map/psum | solution.py:42
  77.6 0.6 broadcast_multiply_fusion.5
  78.2 25.1 %all-reduce.10.cloned.1.call-done = (f32[640,256]{1,0:T(8,128)}, f32[256,640]{0,1:T(8,128)}) async-done(((f32[640,256]{1,0:T(8,128)}, f32[256,640]{0,1:T(8,128)}), (f32[640,256]{1,0:T(8,128)}, f32[256,640]{0,1:T(8,128)})) %all-reduce.10.cloned.1.call-update) | async-done | bytes 1310736 | tf_op jit(solution)/shard_map/psum | solution.py:42
  103.2 0.0 all-reduce.8.cloned.1.call-update
  103.3 0.6 broadcast_multiply_fusion.6
  103.9 3.4 %fusion.21 = bf16[8,256,320]{1,2,0:T(8,128)(2,1)} fusion(bf16[8,320,256]{2,1,0:T(8,128)(2,1)S(1)} %get-tuple-element.31, bf16[8,256,320]{1,2,0:T(8,128)(2,1)S(1)} %copy-done.1, bf16[8,256,320]{1,2,0:T(8,128)(2,1)} %param.8, f32[8,256]{1,0:T(8,128)S(1)} %get-tuple-element.34, f32[8,256]{1,0:T(8,128)S(1)} %get-tuple-element.35, f32[320]{0:T(512)S(1)} %dynamic_slice.6, ...), kind=kLoop, calls=%fused_computation.29 | loop fusion | flops 7864320 | bytes 5276928 | tf_op jit(solution)/shard_map/convert_element_type | solution.py:60
  107.3 56.7 %all-reduce.8.cloned.1.call-done = (f32[640,256]{1,0:T(8,128)}, f32[256,640]{0,1:T(8,128)}) async-done(((f32[640,256]{1,0:T(8,128)}, f32[256,640]{0,1:T(8,128)}), (f32[640,256]{1,0:T(8,128)}, f32[256,640]{0,1:T(8,128)})) %all-reduce.8.cloned.1.call-update) | async-done | bytes 1310736 | tf_op jit(solution)/shard_map/psum | solution.py:42
  164.0 2.0 %broadcast_multiply_fusion.1 = f32[640,256]{1,0:T(8,128)} fusion(f32[640,256]{1,0:T(8,128)} %get-tuple-element.20), kind=kLoop, calls=%fused_computation.46 | loop fusion | flops 163840 | bytes 1310720 | tf_op jit(solution)/shard_map/div | solution.py:63
  166.0 1.1 broadcast_multiply_fusion
  167.1 1.1 copy.13
  (2 shorter events, 0.0 us)
Async XLA Ops:
  7.2 23.9 %copy-start = (bf16[640,256]{1,0:T(8,128)(2,1)S(1)}, bf16[640,256]{1,0:T(8,128)(2,1)}, u32[]{:S(2)}) copy-start(bf16[640,256]{1,0:T(8,128)(2,1)} %param.9) | copy-start | bytes 983044
  7.2 96.1 %all-reduce.10.cloned.1.call-start = ((), (), s32[]{:S(2)}) async-start(), calls=%async_computation.1 | async-start | bytes 2621440 | tf_op jit(solution)/shard_map/psum | solution.py:42
  31.0 2.8 %copy-start.2 = (bf16[8,256,320]{1,2,0:T(8,128)(2,1)S(1)}, bf16[8,256,320]{1,2,0:T(8,128)(2,1)}, u32[]{:S(2)}) copy-start(bf16[8,256,320]{1,2,0:T(8,128)(2,1)} %param.8) | copy-start | bytes 3932164
  31.1 2.8 %copy-start.4 = (f32[640]{0:T(1024)S(1)}, f32[640]{0:T(1024)}, u32[]{:S(2)}) copy-start(f32[640]{0:T(1024)} %param.10) | copy-start | bytes 7684
  33.8 2.4 %copy-start.3 = (bf16[256,640]{1,0:T(8,128)(2,1)S(1)}, bf16[256,640]{1,0:T(8,128)(2,1)}, u32[]{:S(2)}) copy-start(bf16[256,640]{1,0:T(8,128)(2,1)} %param.11) | copy-start | bytes 983044
  36.3 5.5 %copy-start.1 = (bf16[8,256,320]{1,2,0:T(8,128)(2,1)S(1)}, bf16[8,256,320]{1,2,0:T(8,128)(2,1)}, u32[]{:S(2)}) copy-start(bf16[8,256,320]{1,2,0:T(8,128)(2,1)} %param.7) | copy-start | bytes 3932164
  40.1 1.7 copy-start.5
  43.9 120.1 %all-reduce.8.cloned.1.call-start = ((), (), s32[]{:S(2)}) async-start(), calls=%async_computation | async-start | bytes 2621440 | tf_op jit(solution)/shard_map/psum | solution.py:42
Sparse Core Ops, SparseCore 0:
  44.0 59.1 all-reduce.9
  106.5 57.4 all-reduce.7
